TPU v7x, 512 devices: a whole 4x4x16 slice. The times are simulated.
512 devices in a mesh: section: 8 (over x, z_hi), seq: 64 (over y, z_lo, core).
Axes of the slice: x: 4, y: 4, z: 16 (z_hi: 2, z_lo: 8; z = z_hi * 8 + z_lo), core: 2. Of those that a mesh axis runs over, the one named last changes fastest.
Arguments:
- queries: bfloat16 [8, 256, 2048], P('section', 'seq'), may hold values from -120 to 120
- keys_values: bfloat16 [8, 16384, 4096], P('section', 'seq'), may hold values from -41 to 41
- enc_len: int32 [8], P('section'), may hold values from 4096 to 16384, as said below
- order: int32 [8], replicated, may hold values from 0 to 7, each once
- d_out: bfloat16 [8, 256, 2048], P('section', 'seq'), may hold values from -6 to 6
Outputs:
- attended: bfloat16 [8, 256, 2048], P('section', 'seq')
- d_queries: bfloat16 [8, 256, 2048], P('section', 'seq')
- d_keys_values: bfloat16 [8, 16384, 4096], P('section', 'seq')
Inputs may be any that keep to these rules, and one draw needn't show every extreme that they name: Positions from enc_len on are padding; some micro-batch has exactly 16384 valid positions. `order`: every micro-batch is run by exactly one group.
All inputs are finite; a program needn't handle non-finite values.
Results may differ from a plain program's by a relative error of at most 0.0049.
Values may be sent and summed in bfloat16 or wider, within the bound.
A program may use at most 64 MiB of HBM per device.

v0:
```python
import math
import jax
import jax.numpy as jnp
from jax import lax
from jax.sharding import PartitionSpec as P

HD = 256


def combined_all(shard, axis, combine):
    everything = jax.tree.map(lambda part: lax.all_gather(part, axis), shard)
    initial = jax.tree.map(lambda part: part[0], everything)

    def step(k, so_far):
        return combine(so_far, jax.tree.map(lambda part: part[k], everything))

    return lax.fori_loop(1, lax.axis_size(axis), step, initial)


def combine_stats(first, second):
    top = jnp.maximum(first[0], second[0])
    total = first[1] * jnp.exp(first[0] - top) + second[1] * jnp.exp(second[0] - top)
    return (top, total)


def shards(queries, keys_values, enc_len, order, d_out):
    score_scale = 1.0 / math.sqrt(HD)
    section_count = lax.axis_size("section")
    my_section = lax.axis_index("section")
    seq_index = lax.axis_index("seq")
    slots = jnp.arange(section_count, dtype=jnp.int32)
    my_batch = jnp.sum(jnp.where(slots == my_section, order, 0))
    source = jnp.sum(jnp.where(order == my_section, slots, 0))
    to_batch = (slots == my_batch)[:, None, None]
    zero_bf = jnp.zeros((), jnp.bfloat16)
    query_send = jnp.where(to_batch, queries[0][None], zero_bf)
    grad_send = jnp.where(to_batch, d_out[0][None], zero_bf)
    query_recv, grad_recv = (
        lax.all_to_all(query_send, "section", split_axis=0, concat_axis=0, tiled=True),
        lax.all_to_all(grad_send, "section", split_axis=0, concat_axis=0, tiled=True),
    )
    query_local = jnp.sum(query_recv, axis=0, dtype=jnp.bfloat16)
    grad_local = jnp.sum(grad_recv, axis=0, dtype=jnp.bfloat16)
    query_all, grad_all = (
        lax.all_gather(query_local, "seq", axis=0, tiled=True),
        lax.all_gather(grad_local, "seq", axis=0, tiled=True),
    )
    local_rows = keys_values.shape[1]
    tq_rows = queries.shape[1]
    attn_width = keys_values.shape[2] // 2
    head_count = attn_width // HD
    memory = keys_values[0]
    key_heads = memory[:, :attn_width].reshape(local_rows, head_count, HD)
    value_heads = memory[:, attn_width:].reshape(local_rows, head_count, HD)
    query_heads = query_all.reshape(-1, head_count, HD)
    grad_heads = grad_all.reshape(-1, head_count, HD)
    length = enc_len[0]
    first_key = seq_index * local_rows
    key_valid = jnp.arange(local_rows, dtype=jnp.int32) + first_key < length
    scores = (
        jnp.einsum("ihd,jhd->hij", query_heads, key_heads, preferred_element_type=jnp.float32)
        * score_scale
    )
    scores = jnp.where(key_valid[None, None, :], scores, -jnp.inf)
    local_max = jnp.maximum(jnp.max(scores, axis=-1), -1e30)
    local_sum = jnp.sum(jnp.exp(scores - local_max[..., None]), axis=-1)
    whole_max, whole_sum = combined_all((local_max, local_sum), "seq", combine_stats)
    probabilities = jnp.exp(scores - whole_max[..., None]) / whole_sum[..., None]
    weights = probabilities.astype(jnp.bfloat16)
    result = jnp.einsum("hij,jhd->ihd", weights, value_heads, preferred_element_type=jnp.float32)
    attended_sum = lax.psum_scatter(
        result.reshape(tq_rows * lax.axis_size("seq"), attn_width),
        "seq",
        scatter_dimension=0,
        tiled=True,
    )
    dprobs = jnp.einsum("ihd,jhd->hij", grad_heads, value_heads, preferred_element_type=jnp.float32)
    delta = lax.psum(jnp.sum(probabilities * dprobs, axis=-1), "seq")
    dscores = (probabilities * (dprobs - delta[..., None]) * score_scale).astype(jnp.bfloat16)
    result = jnp.einsum("hij,jhd->ihd", dscores, key_heads, preferred_element_type=jnp.float32)
    query_sum = lax.psum_scatter(
        result.reshape(tq_rows * lax.axis_size("seq"), attn_width),
        "seq",
        scatter_dimension=0,
        tiled=True,
    )
    attended = attended_sum.astype(jnp.bfloat16)
    d_queries = query_sum.astype(jnp.bfloat16)
    key_grad = jnp.einsum("hij,ihd->jhd", dscores, query_heads, preferred_element_type=jnp.float32)
    value_grad = jnp.einsum("hij,ihd->jhd", weights, grad_heads, preferred_element_type=jnp.float32)
    joined = jnp.concatenate(
        [key_grad.reshape(local_rows, attn_width), value_grad.reshape(local_rows, attn_width)],
        axis=1,
    )
    d_memory = joined.astype(jnp.bfloat16)
    to_source = (slots == source)[:, None, None]
    attended_back = jnp.where(to_source, attended[None], zero_bf)
    queries_back = jnp.where(to_source, d_queries[None], zero_bf)
    attended_home, queries_home = (
        lax.all_to_all(attended_back, "section", split_axis=0, concat_axis=0, tiled=True),
        lax.all_to_all(queries_back, "section", split_axis=0, concat_axis=0, tiled=True),
    )
    attended_out = jnp.sum(attended_home, axis=0, dtype=jnp.bfloat16)
    queries_out = jnp.sum(queries_home, axis=0, dtype=jnp.bfloat16)
    return (attended_out[None], queries_out[None], d_memory[None])


def solution(mesh):
    placed = (
        P("section", "seq", None),
        P("section", "seq", None),
        P("section"),
        P(),
        P("section", "seq", None),
    )
    return jax.shard_map(
        shards,
        mesh=mesh,
        in_specs=placed,
        out_specs=(P("section", "seq", None), P("section", "seq", None), P("section", "seq", None)),
        check_vma=False,
    )
```

profile of v0, /device:TPU:2, one launch (start us, length us, event | category | flops | bytes accessed | tf_op | source)
XLA Modules:
  0.0 1204.9 jit_solution(6223347452346712044)
XLA Ops:
  7.2 1.3 fusion.6
  8.5 1.3 iota_compare_fusion
  9.8 1.6 broadcast_select_fusion
  11.4 31.6 %all_to_all.20 = bf16[8,4,2048]{2,1,0:T(4,128)(2,1)S(1)} all-to-all(bf16[8,4,2048]{2,1,0:T(4,128)(2,1)S(1)} %get-tuple-element.159), channel_id=1, replica_groups=mesh['section'=8,'seq'=64] {'section'}, dimensions={0} | all-to-all | bytes 262144 | tf_op jit(solution)/shard_map/all_to_all | solution.py:39
  43.7 4.9 all-to-all-start.2
  48.6 3.3 copy.86
  52.6 1.3 dynamic-slice
  54.6 1.5 fusion.7
  56.1 6.4 all-to-all-done.2
  63.2 95.6 %all-gather.7.cloned.1.call-done = bf16[64,4,2048]{2,1,0:T(4,128)(2,1)} async-done(((bf16[1,4,2048]{2,1,0:T(4,128)(2,1)}), bf16[64,4,2048]{2,1,0:T(4,128)(2,1)}) %all-gather.7.cloned.1.call-update) | async-done | bytes 1048592 | tf_op jit(solution)/shard_map/all_gather | solution.py:45
  158.8 1.8 reshape.89
  160.6 0.8 copy.98
  161.4 1.8 fusion.8
  163.3 118.9 %all-gather = f32[512,256]{1,0:T(8,128)S(1)} all-gather(f32[8,256]{1,0:T(8,128)S(1)} %broadcast_maximum_fusion), channel_id=2, replica_groups=mesh['section'=8,'seq'=64] {'seq'}, dimensions={0}, use_global_device_ids=true | all-gather | bytes 532480 | tf_op jit(solution)/shard_map/all_gather | solution.py:11
  282.5 114.5 %all-gather.1 = f32[512,256]{1,0:T(8,128)S(1)} all-gather(f32[8,256]{1,0:T(8,128)S(1)} %exponential_reduce_fusion), channel_id=3, replica_groups=mesh['section'=8,'seq'=64] {'seq'}, dimensions={0}, use_global_device_ids=true | all-gather | bytes 532480 | tf_op jit(solution)/shard_map/all_gather | solution.py:11
  397.0 0.8 copy-done.7
  397.8 47.4 %while.17 = (s32[]{:T(128)}, f32[8,256]{1,0:T(8,128)S(1)}, f32[8,256]{1,0:T(8,128)S(1)}, f32[64,8,256]{2,1,0:T(8,128)}, f32[64,8,256]{2,1,0:T(8,128)}, /*index=5*/s32[]{:T(128)}, s32[]{:T(128)}, s32[]{:T(128)}) while((s32[]{:T(128)}, f32[8,256]{1,0:T(8,128)S(1)}, f32[8,256]{1,0:T(8,128)S(1)}, f32[64,8,256]{2,1,0:T(8,128)}, ...), condition=%wide.region_6.7_spmd, body=%wide.region_5.6_spmd.sunk | while | flops 12293 | bytes 49283 | solution.py:17
  398.5 0.7 fusion.21
  399.3 0.7 fusion.21
  400.1 0.7 fusion.21
  401.6 0.7 fusion.21
  402.3 0.7 fusion.21
  403.1 0.7 fusion.21
  404.6 0.7 fusion.21
  405.3 0.7 fusion.21
  406.1 0.7 fusion.21
  407.6 0.7 fusion.21
  409.1 0.7 fusion.21
  410.6 0.7 fusion.21
  411.4 0.7 fusion.21
  412.9 0.7 fusion.21
  414.4 0.7 fusion.21
  415.1 0.7 fusion.21
  415.9 0.7 fusion.21
  416.6 0.7 fusion.21
  418.1 0.7 fusion.21
  419.6 0.7 fusion.21
  420.4 0.7 fusion.21
  421.9 0.7 fusion.21
  423.4 0.7 fusion.21
  424.9 0.7 fusion.21
  425.7 0.7 fusion.21
  443.0 0.7 fusion.21
  444.5 0.7 fusion.21
  445.3 2.6 reshape.93
  447.8 2.4 copy.100
  450.2 3.2 fusion.3
  453.5 2.0 multiply_reduce_fusion
  455.5 214.0 %psum.7 = f32[8,256]{1,0:T(8,128)S(1)} all-reduce(f32[8,256]{1,0:T(8,128)S(1)} %get-tuple-element.162), channel_id=1, replica_groups=mesh['section'=8,'seq'=64] {'seq'}, use_global_device_ids=true, to_apply=%region_11.12 | all-reduce | flops 2048 | bytes 16384 | tf_op jit(solution)/shard_map/psum | solution.py:78
  669.5 2.2 multiply_convert_fusion
  671.8 1.8 fusion.9
  673.6 470.9 %all-reduce.4 = (bf16[256,2048]{0,1:T(8,128)(2,1)}, bf16[256,2048]{0,1:T(8,128)(2,1)}) all-reduce(f32[256,2048]{0,1:T(8,128)} %bitcast.59, f32[256,2048]{0,1:T(8,128)} %bitcast.57), channel_id=4, replica_groups=mesh['section'=8,'seq'=64] {'seq'}, use_global_device_ids=true, to_apply=%region_7.8.clone | all-reduce | flops 1048576 | bytes 6291456
  1144.4 2.0 constant_dynamic-slice_fusion.1
  1146.5 1.2 copy.90
  1147.7 2.1 constant_dynamic-slice_fusion
  1149.8 1.2 copy.96
  1151.0 0.9 broadcast_select_fusion.2
  1151.9 10.9 all-to-all-start.1
  1162.9 2.8 convolution_convert_fusion
  1165.7 2.4 copy.103
  1169.2 7.5 all-to-all-done.1
  1176.7 7.0 all-to-all-start.3
  1183.6 1.5 pad_maximum_fusion
  1185.7 11.7 all-to-all-done.3
  (67 shorter events, 30.5 us)
Async XLA Ops:
  7.2 151.7 %all-gather.7.cloned.1.call-start = ((), (), s32[]{:S(2)}) async-start(), calls=%async_computation.4 | async-start | bytes 1064960 | tf_op jit(solution)/shard_map/all_gather | solution.py:45
  43.7 18.8 %all-to-all-start.2 = ((bf16[8,4,2048]{2,1,0:T(4,128)(2,1)}), bf16[8,4,2048]{2,1,0:T(4,128)(2,1)S(1)}, u32[]{:S(2)}, u32[]{:S(2)}) async-start(bf16[8,4,2048]{2,1,0:T(4,128)(2,1)} %get-tuple-element.158), calls=%async_computation.2 | async-start | bytes 262144 | tf_op jit(solution)/shard_map/all_to_all | solution.py:40
  48.6 396.6 %all-gather.9.cloned.1.call-start = ((), (), s32[]{:S(2)}) async-start(), calls=%async_computation.5 | async-start | bytes 1064960 | tf_op jit(solution)/shard_map/all_gather | solution.py:46
  282.2 114.8 %copy-start.6 = (f32[512,256]{1,0:T(8,128)}, f32[512,256]{1,0:T(8,128)S(1)}, u32[]{:S(2)}) copy-start(f32[512,256]{1,0:T(8,128)S(1)} %all-gather) | copy-start | bytes 1572868
  397.0 0.8 copy-start.7
  450.2 3.2 copy-start.4
  450.2 3.2 copy-start.5
  669.5 2.2 copy-start.2
  671.7 1.8 copy-start
  1151.9 24.7 %all-to-all-start.1 = ((bf16[8,4,2048]{2,1,0:T(4,128)(2,1)}), bf16[8,4,2048]{2,1,0:T(4,128)(2,1)S(1)}, u32[]{:S(2)}, u32[]{:S(2)}) async-start(bf16[8,4,2048]{2,1,0:T(4,128)(2,1)} %get-tuple-element.157), calls=%async_computation.1 | async-start | bytes 262144 | tf_op jit(solution)/shard_map/all_to_all | solution.py:100
  1165.7 2.4 copy-start.1
  1168.5 15.1 %copy-start.3 = (bf16[1,256,2048]{2,1,0:T(8,128)(2,1)S(1)}, bf16[1,256,2048]{2,1,0:T(8,128)(2,1)}, u32[]{:S(2)}) copy-start(bf16[1,256,2048]{2,1,0:T(8,128)(2,1)} %copy.103) | copy-start | bytes 3145732
  1176.7 20.7 %all-to-all-start.3 = ((bf16[8,4,2048]{2,1,0:T(4,128)(2,1)}), bf16[8,4,2048]{2,1,0:T(4,128)(2,1)S(1)}, u32[]{:S(2)}, u32[]{:S(2)}) async-start(bf16[8,4,2048]{2,1,0:T(4,128)(2,1)} %get-tuple-element.156), calls=%async_computation.3 | async-start | bytes 262144 | tf_op jit(solution)/shard_map/all_to_all | solution.py:101
Sparse Core Ops, SparseCore 0:
  43.8 114.9 all-gather.6
  161.5 115.5 all-gather.8
where the time goes:
time: 1210 us; the launch traced here: 1200 us
  blocking collectives  950 us (79%)
  waiting for transfers between devices  121 us (10%)
  other arithmetic  57.8 us (5%)
  local copies, waits for them, and re-layouts  24.1 us (2%)
  starting transfers between devices  22.9 us (2%)
  between operations  15.5 us (1%)
  matrix products  12.1 us (1%)
    unnamed x1, blocking collectives  471 us
    all_gather x2, blocking collectives, combined_all(): everything = jax.tree.map(lambda part: lax.all_gather(part, axis), shard)  233 us
    psum x1, blocking collectives, shards(): delta = lax.psum(jnp.sum(probabilities * dprobs, axis=-1), 'seq')  214 us
    all_gather x1, waiting for transfers between devices, shards(): lax.all_gather(query_local, 'seq', axis=0, tiled=True)  95.6 us
    add x63, other arithmetic, combine_stats(): first[1] * jnp.exp(first[0] - top) + second[1] * jnp.exp(second[0] - top)  46.1 us
    all_to_all x1, blocking collectives, shards(): lax.all_to_all(query_send, 'section', split_axis=0, concat_axis=0, tiled=...  31.6 us
  transfers between devices with their start and end apart: 5, of which 4 were waited for; matrix products, arithmetic and copies ran while one was open for 5% of the time, Pallas kernels for 0%

commit v1 on v0

--- a/solution.py
+++ b/solution.py
@@ -75,7 +75,7 @@
         tiled=True,
     )
     dprobs = jnp.einsum("ihd,jhd->hij", grad_heads, value_heads, preferred_element_type=jnp.float32)
-    delta = lax.psum(jnp.sum(probabilities * dprobs, axis=-1), "seq")
+    delta = jnp.sum(lax.all_gather(jnp.sum(probabilities * dprobs, axis=-1), "seq"), axis=0)
     dscores = (probabilities * (dprobs - delta[..., None]) * score_scale).astype(jnp.bfloat16)
     result = jnp.einsum("hij,jhd->ihd", dscores, key_heads, preferred_element_type=jnp.float32)
     query_sum = lax.psum_scatter(

time: 1210 us -> 1110 us (0.917)
  blocking collectives: 950 us -> 852 us
    psum x1 -> x0, blocking collectives: 214 us -> none  [shards(): delta = lax.psum(jnp.sum(probabilities * dprobs, axis=-1), 'seq')]
    all_gather x0 -> x1, blocking collectives: none -> 116 us  [shards(): lax.all_gather(jnp.sum(probabilities * dprobs, axis=-1), 'seq')]
  transfers between devices with their start and end apart: 5 -> 5, of which waited for: 4 -> 4; matrix products, arithmetic and copies ran while one was open for 5% -> 6% of each run, Pallas kernels for 0% -> 0%
where the time goes in v1:
time: 1110 us; the launch traced here: 1100 us
  blocking collectives  852 us (77%)
  waiting for transfers between devices  121 us (11%)
  other arithmetic  56.2 us (5%)
  local copies, waits for them, and re-layouts  24.7 us (2%)
  starting transfers between devices  22.7 us (2%)
  between operations  15.5 us (1%)
    unnamed x1, blocking collectives  471 us
    all_gather x2, blocking collectives, combined_all(): everything = jax.tree.map(lambda part: lax.all_gather(part, axis), shard)  233 us
    all_gather x1, blocking collectives, shards(): lax.all_gather(jnp.sum(probabilities * dprobs, axis=-1), 'seq')  116 us
    all_gather x1, waiting for transfers between devices, shards(): lax.all_gather(query_local, 'seq', axis=0, tiled=True)  95.6 us
    add x63, other arithmetic, combine_stats(): first[1] * jnp.exp(first[0] - top) + second[1] * jnp.exp(second[0] - top)  46.1 us
    all_to_all x1, blocking collectives, shards(): lax.all_to_all(query_send, 'section', split_axis=0, concat_axis=0, tiled=...  31.6 us
  transfers between devices with their start and end apart: 5, of which 4 were waited for; matrix products, arithmetic and copies ran while one was open for 6% of the time, Pallas kernels for 0%

profile of v1, /device:TPU:2, one launch (start us, length us, event | category | flops | bytes accessed | tf_op | source)
XLA Modules:
  0.0 1104.9 jit_solution(12918390950696734801)
XLA Ops:
  7.2 1.3 fusion.6
  8.5 1.3 iota_compare_fusion
  9.8 1.6 broadcast_select_fusion
  11.4 31.6 %all_to_all.20 = bf16[8,4,2048]{2,1,0:T(4,128)(2,1)S(1)} all-to-all(bf16[8,4,2048]{2,1,0:T(4,128)(2,1)S(1)} %get-tuple-element.159), channel_id=1, replica_groups=mesh['section'=8,'seq'=64] {'section'}, dimensions={0} | all-to-all | bytes 262144 | tf_op jit(solution)/shard_map/all_to_all | solution.py:39
  43.7 4.9 all-to-all-start.2
  48.6 3.3 copy.86
  52.6 1.3 dynamic-slice
  54.6 1.5 fusion.7
  56.1 6.4 all-to-all-done.2
  63.2 95.6 %all-gather.8.cloned.1.call-done = bf16[64,4,2048]{2,1,0:T(4,128)(2,1)} async-done(((bf16[1,4,2048]{2,1,0:T(4,128)(2,1)}), bf16[64,4,2048]{2,1,0:T(4,128)(2,1)}) %all-gather.8.cloned.1.call-update) | async-done | bytes 1048592 | tf_op jit(solution)/shard_map/all_gather | solution.py:45
  158.8 1.8 reshape.89
  160.6 0.8 copy.98
  161.4 1.8 fusion.8
  163.3 118.9 %all-gather = f32[512,256]{1,0:T(8,128)S(1)} all-gather(f32[8,256]{1,0:T(8,128)S(1)} %broadcast_maximum_fusion), channel_id=2, replica_groups=mesh['section'=8,'seq'=64] {'seq'}, dimensions={0}, use_global_device_ids=true | all-gather | bytes 532480 | tf_op jit(solution)/shard_map/all_gather | solution.py:11
  282.5 114.5 %all-gather.1 = f32[512,256]{1,0:T(8,128)S(1)} all-gather(f32[8,256]{1,0:T(8,128)S(1)} %exponential_reduce_fusion), channel_id=3, replica_groups=mesh['section'=8,'seq'=64] {'seq'}, dimensions={0}, use_global_device_ids=true | all-gather | bytes 532480 | tf_op jit(solution)/shard_map/all_gather | solution.py:11
  397.0 0.8 copy-done.7
  397.8 47.4 %while.17 = (s32[]{:T(128)}, f32[8,256]{1,0:T(8,128)S(1)}, f32[8,256]{1,0:T(8,128)S(1)}, f32[64,8,256]{2,1,0:T(8,128)}, f32[64,8,256]{2,1,0:T(8,128)}, /*index=5*/s32[]{:T(128)}, s32[]{:T(128)}, s32[]{:T(128)}) while((s32[]{:T(128)}, f32[8,256]{1,0:T(8,128)S(1)}, f32[8,256]{1,0:T(8,128)S(1)}, f32[64,8,256]{2,1,0:T(8,128)}, ...), condition=%wide.region_6.7_spmd, body=%wide.region_5.6_spmd.sunk | while | flops 12293 | bytes 49283 | solution.py:17
  398.5 0.7 fusion.21
  399.3 0.7 fusion.21
  400.1 0.7 fusion.21
  401.6 0.7 fusion.21
  402.3 0.7 fusion.21
  403.1 0.7 fusion.21
  404.6 0.7 fusion.21
  405.3 0.7 fusion.21
  406.1 0.7 fusion.21
  407.6 0.7 fusion.21
  409.1 0.7 fusion.21
  410.6 0.7 fusion.21
  411.4 0.7 fusion.21
  412.9 0.7 fusion.21
  414.4 0.7 fusion.21
  415.1 0.7 fusion.21
  415.9 0.7 fusion.21
  416.6 0.7 fusion.21
  418.1 0.7 fusion.21
  419.6 0.7 fusion.21
  420.4 0.7 fusion.21
  421.9 0.7 fusion.21
  423.4 0.7 fusion.21
  424.9 0.7 fusion.21
  425.7 0.7 fusion.21
  427.2 0.7 fusion.21
  443.0 0.7 fusion.21
  444.5 0.7 fusion.21
  445.3 2.6 reshape.93
  447.8 2.4 copy.100
  450.2 3.2 fusion.3
  453.5 0.8 multiply_reduce_fusion
  454.3 116.0 %all-gather.2 = f32[512,256]{1,0:T(8,128)S(1)} all-gather(f32[8,256]{1,0:T(8,128)S(1)} %get-tuple-element.162), channel_id=4, replica_groups=mesh['section'=8,'seq'=64] {'seq'}, dimensions={0}, use_global_device_ids=true | all-gather | bytes 532480 | tf_op jit(solution)/shard_map/all_gather | solution.py:78
  571.5 1.8 fusion.9
  573.3 471.3 %all-reduce.4 = (bf16[256,2048]{0,1:T(8,128)(2,1)}, bf16[256,2048]{0,1:T(8,128)(2,1)}) all-reduce(f32[256,2048]{0,1:T(8,128)} %bitcast.61, f32[256,2048]{0,1:T(8,128)} %bitcast.59), channel_id=5, replica_groups=mesh['section'=8,'seq'=64] {'seq'}, use_global_device_ids=true, to_apply=%region_7.8.clone | all-reduce | flops 1048576 | bytes 6291456
  1044.6 2.0 constant_dynamic-slice_fusion.1
  1046.7 1.2 copy.90
  1047.9 2.1 constant_dynamic-slice_fusion
  1050.0 1.2 copy.96
  1051.2 0.9 broadcast_select_fusion.2
  1052.1 10.7 all-to-all-start.1
  1062.8 2.8 convolution_convert_fusion
  1065.6 2.4 copy.103
  1069.1 7.5 all-to-all-done.1
  1076.6 7.0 all-to-all-start.3
  1083.6 1.5 pad_maximum_fusion
  1085.7 11.7 %all-to-all-done.3 = bf16[8,4,2048]{2,1,0:T(4,128)(2,1)S(1)} async-done(((bf16[8,4,2048]{2,1,0:T(4,128)(2,1)}), bf16[8,4,2048]{2,1,0:T(4,128)(2,1)S(1)}, u32[]{:S(2)}, u32[]{:S(2)}) %all-to-all-start.3) | async-done | bytes 131104 | tf_op jit(solution)/shard_map/all_to_all | solution.py:101
  (68 shorter events, 31.1 us)
Async XLA Ops:
  7.2 151.7 %all-gather.8.cloned.1.call-start = ((), (), s32[]{:S(2)}) async-start(), calls=%async_computation.4 | async-start | bytes 1064960 | tf_op jit(solution)/shard_map/all_gather | solution.py:45
  43.7 18.8 %all-to-all-start.2 = ((bf16[8,4,2048]{2,1,0:T(4,128)(2,1)}), bf16[8,4,2048]{2,1,0:T(4,128)(2,1)S(1)}, u32[]{:S(2)}, u32[]{:S(2)}) async-start(bf16[8,4,2048]{2,1,0:T(4,128)(2,1)} %get-tuple-element.158), calls=%async_computation.2 | async-start | bytes 262144 | tf_op jit(solution)/shard_map/all_to_all | solution.py:40
  48.6 396.6 %all-gather.10.cloned.1.call-start = ((), (), s32[]{:S(2)}) async-start(), calls=%async_computation.5 | async-start | bytes 1064960 | tf_op jit(solution)/shard_map/all_gather | solution.py:46
  282.2 114.8 %copy-start.6 = (f32[512,256]{1,0:T(8,128)}, f32[512,256]{1,0:T(8,128)S(1)}, u32[]{:S(2)}) copy-start(f32[512,256]{1,0:T(8,128)S(1)} %all-gather) | copy-start | bytes 1572868
  397.0 0.8 copy-start.7
  450.2 3.2 copy-start.4
  450.2 3.2 copy-start.5
  570.3 1.2 copy-start.2
  571.5 1.8 copy-start
  1052.1 24.5 %all-to-all-start.1 = ((bf16[8,4,2048]{2,1,0:T(4,128)(2,1)}), bf16[8,4,2048]{2,1,0:T(4,128)(2,1)S(1)}, u32[]{:S(2)}, u32[]{:S(2)}) async-start(bf16[8,4,2048]{2,1,0:T(4,128)(2,1)} %get-tuple-element.157), calls=%async_computation.1 | async-start | bytes 262144 | tf_op jit(solution)/shard_map/all_to_all | solution.py:100
  1065.6 2.4 copy-start.1
  1068.5 15.1 %copy-start.3 = (bf16[1,256,2048]{2,1,0:T(8,128)(2,1)S(1)}, bf16[1,256,2048]{2,1,0:T(8,128)(2,1)}, u32[]{:S(2)}) copy-start(bf16[1,256,2048]{2,1,0:T(8,128)(2,1)} %copy.103) | copy-start | bytes 3145732
  1076.6 20.7 %all-to-all-start.3 = ((bf16[8,4,2048]{2,1,0:T(4,128)(2,1)}), bf16[8,4,2048]{2,1,0:T(4,128)(2,1)S(1)}, u32[]{:S(2)}, u32[]{:S(2)}) async-start(bf16[8,4,2048]{2,1,0:T(4,128)(2,1)} %get-tuple-element.156), calls=%async_computation.3 | async-start | bytes 262144 | tf_op jit(solution)/shard_map/all_to_all | solution.py:101
Sparse Core Ops, SparseCore 0:
  43.8 114.9 all-gather.7
  161.5 115.5 all-gather.9
